TPU v7x, 128 devices: a whole 4x4x4 slice. The times are simulated.
128 devices in a mesh: row: 16 (over z_lo, y, core), col: 8 (over x, z_hi).
Axes of the slice: x: 4, y: 4, z: 4 (z_hi: 2, z_lo: 2; z = z_hi * 2 + z_lo), core: 2. Of those that a mesh axis runs over, the one named last changes fastest.
Arguments:
- queries: bfloat16 [8, 128, 4096], P(None, 'row', 'col'), may hold values from -13 to 13, as said below
- key_cache: bfloat16 [8, 65536, 1024], P(None, ('row', 'col')), may hold values from -13 to 13
- value_cache: bfloat16 [8, 65536, 1024], P(None, ('row', 'col')), may hold values from -6 to 6
- key_table: bfloat16 [1024, 1024], replicated, may hold values from -24 to 24
- value_table: bfloat16 [1024, 1024], replicated, may hold values from -6 to 6
- lengths: int32 [8], replicated, may hold values from 8192 to 65536
- token_ids: int32 [8, 128], P(None, 'row'), may hold values from 0 to 1023
Outputs:
- attended: bfloat16 [8, 128, 4096], P(None, 'row', 'col')
Inputs may be any that keep to these rules, and one draw needn't show every extreme that they name: `queries`: entries of the query array lie in the stated range.
All inputs are finite; a program needn't handle non-finite values.
Results may differ from a plain program's by a relative error of at most 0.006.
Values may be sent and summed in bfloat16 or wider, within the bound.
No kernel may reach another device: no remote copies, remote signals or barrier semaphores. Data moves between devices by JAX's collectives and lax.ppermute only.
A program may use at most 192 MiB of HBM per device.

v0:
```python
import functools

import jax
import jax.numpy as jnp
import numpy as np
from jax import lax
from jax.experimental import pallas as pl
from jax.experimental.pallas import tpu as pltpu
from jax.sharding import Mesh
from jax.sharding import PartitionSpec as P

KH = 8
GROUP = 4
HD = 128
HALF = HD // 2
SCALE2 = HD**-0.5 * 1.4426950408889634
FINE = ("zl", "y", "c", "x", "zh")
SIZES = (2, 4, 2, 4, 2)
CHIPS = ("zl", "y", "x", "zh")
DEAD = -(2.0**100)
ROWS = 64
META = 8
PARTS = 2


def packed_tiles(first, second):
    low = lax.broadcasted_iota(jnp.int32, (first.shape[0], HD), 1) < ROWS
    out = []
    for k in range(first.shape[1] // HD):
        a = first[:, k * HD : (k + 1) * HD]
        b = second[:, k * HD : (k + 1) * HD]
        crossed = pltpu.roll(jnp.where(low, b, a), ROWS, 1)
        out.append(jnp.where(low, a, crossed))
        out.append(jnp.where(low, crossed, b))
    return out


def partial_kernel(step, asks, results, info, lengths, *refs):
    q_refs = refs[:asks]
    k0_ref, k1_ref, v0_ref, v1_ref = refs[asks : asks + 4]
    length = k0_ref.shape[1]
    heads = q_refs[0].shape[1]
    leads = sum(r.shape[0] for r in q_refs)
    o_refs = refs[len(refs) - results :]
    each = leads // len(o_refs)
    width = leads * ROWS
    user = (info[1] + (KH - step)) % (lengths.shape[0] // 2)
    limit0 = lengths[info[0] + user] - info[2]
    limit1 = lengths[info[0] + user] - info[3]
    limits = (limit0, limit1)
    rows_dims = (((1,), (1,)), ((), ()))
    first_dims = (((0,), (0,)), ((), ()))

    def columns(j):
        if isinstance(j, int):
            return slice(j * HD, (j + 1) * HD)
        return pl.ds(pl.multiple_of(j * HD, HD), HD)

    def scores(j):
        cols = columns(j)
        q = [r[:, j].reshape(r.shape[0] * ROWS, HD) for r in q_refs]
        q = jnp.concatenate(q) if len(q) > 1 else q[0]
        return [
            lax.dot_general(k[0, :, cols], q, rows_dims, preferred_element_type=jnp.float32)
            for k in (k0_ref, k1_ref)
        ]

    def weights(s, masked):
        s = [part * SCALE2 for part in s]
        if masked:
            at = lax.broadcasted_iota(jnp.int32, (length, width), 0)
            s = [jnp.where(at < limit, part, DEAD) for limit, part in zip(limits, s)]
        peak = jnp.maximum(*[jnp.max(part, axis=0, keepdims=True) for part in s])
        peak = peak.astype(jnp.bfloat16).astype(jnp.float32)
        w = [jnp.exp2(part - peak) for part in s]
        total = sum(jnp.sum(part, axis=0, keepdims=True) for part in w)
        return [part.astype(jnp.bfloat16) for part in w], total, peak

    def store(j, w, total, peak):
        cols = columns(j)
        numer = sum(
            lax.dot_general(
                v[0, :, cols], part, first_dims, preferred_element_type=jnp.float32
            )
            for v, part in zip((v0_ref, v1_ref), w)
        )
        numer = numer * (1.0 / total)
        high = total.astype(jnp.bfloat16).astype(jnp.float32)
        low = total - high
        top = lax.broadcasted_iota(jnp.int32, (META, width), 0) == 0
        tiles = packed_tiles(numer[:HALF], numer[HALF:])
        notes = packed_tiles(jnp.where(top, peak, low), jnp.where(top, high, low))
        for d in range(leads):
            o_refs[d // each][d % each, j, :ROWS, :] = tiles[d].astype(jnp.bfloat16)
            o_refs[d // each][d % each, j, ROWS:, :] = notes[d].astype(jnp.bfloat16)

    live = (limit0 >= length) & (limit1 >= length)

    @pl.when(live)
    def _():
        s = scores(0)
        for j in range(heads):
            ahead = scores(j + 1) if j + 1 < heads else None
            store(j, *weights(s, False))
            s = ahead

    dead = (limit0 <= 0) & (limit1 <= 0)

    @pl.when(dead)
    def _():
        shape = (heads, META, HD)
        side = lax.broadcasted_iota(jnp.int32, shape, 2) < ROWS
        first = lax.broadcasted_iota(jnp.int32, shape, 1) == 0
        note = jnp.where(first, jnp.where(side, DEAD, 1.0), 0.0).astype(jnp.bfloat16)
        for d in range(leads):
            empty = jnp.zeros((heads, ROWS, HD), jnp.bfloat16)
            o_refs[d // each][d % each, :, :ROWS, :] = empty
            o_refs[d // each][d % each, :, ROWS:, :] = note

    @pl.when(jnp.logical_not(live | dead))
    def _():
        @pl.loop(0, heads)
        def _(j):
            store(j, *weights(scores(j), True))


def partials(step, info, lengths, asked, caches, results=1, parts=(0, PARTS), into=()):
    heads = asked[0].shape[1]
    lead = sum(q.shape[0] for q in asked)
    length = caches[0].shape[1]
    share = heads // PARTS
    begin, steps = parts
    half = lengths.shape[0] // 2

    def mine(p, info, lengths):
        return (info[0] + (info[1] + (KH - step)) % half, 0, begin + p)

    def other(p, info, lengths):
        return ((info[1] + (KH - step)) % half, 0, begin + p)

    def heads_at(p, info, lengths):
        return (0, begin + p, 0, 0)

    cache = (1, length, share * HD)
    each = lead // results
    out = jax.ShapeDtypeStruct((each, heads, ROWS + META, HD), jnp.bfloat16)
    return pl.pallas_call(
        functools.partial(partial_kernel, step, len(asked), results),
        grid_spec=pltpu.PrefetchScalarGridSpec(
            num_scalar_prefetch=2,
            grid=(steps,),
            in_specs=[pl.BlockSpec((q.shape[0], share, ROWS, HD), heads_at) for q in asked]
            + [pl.BlockSpec(cache, mine), pl.BlockSpec(cache, other)] * 2
            + [pl.BlockSpec(memory_space=pl.ANY)] * len(into),
            out_specs=[pl.BlockSpec((each, share, ROWS + META, HD), heads_at)] * results,
        ),
        out_shape=[out] * results,
        input_output_aliases={6 + len(asked) + i: i for i in range(len(into))},
        compiler_params=pltpu.CompilerParams(
            dimension_semantics=("arbitrary",),
            vmem_limit_bytes=60 << 20,
        ),
        cost_estimate=pl.CostEstimate(
            flops=8 * share * steps * lead * ROWS * HD * length,
            bytes_accessed=8 * length * share * steps * HD,
            transcendentals=2 * share * steps * lead * ROWS * length,
        ),
    )(info, lengths, *asked, *caches, *into)


def stats_of(notes, low):
    line = notes[:1]
    turned = pltpu.roll(line, ROWS, 1)
    return jnp.where(low, line, turned), jnp.where(low, turned, line) + notes[1:2]


def merge_kernel(cuts, *refs):
    o_ref, w_ref = refs[-2:]
    count = o_ref.shape[0]
    low = lax.broadcasted_iota(jnp.int32, (8, HD), 1) < ROWS
    first = lax.broadcasted_iota(jnp.int32, (8, META, HD), 1) == 0

    def join(parts):
        def note(i, _):
            at = pl.ds(pl.multiple_of(i * 8, 8), 8)
            peaks, masses = [], []
            for r, base in parts:
                notes = r[pl.ds(pl.multiple_of(base + i * 8, 8), 8), ROWS:, :].astype(jnp.float32)
                line = notes[:, 0, :]
                turned = pltpu.roll(line, ROWS, 1)
                peaks.append(jnp.where(low, line, turned))
                masses.append(jnp.where(low, turned, line) + notes[:, 1, :])
            peak = functools.reduce(jnp.maximum, peaks)
            weights = [m * jnp.exp2(p - peak) for p, m in zip(peaks, masses)]
            total = functools.reduce(jnp.add, weights)
            inverse = 1.0 / total
            for n, w in enumerate(weights):
                w_ref[n, at, :] = w * inverse
            high = total.astype(jnp.bfloat16).astype(jnp.float32)
            line = jnp.where(low, peak, high)
            rest = total - high
            o_ref[at, ROWS:, :] = jnp.where(first, line[:, None], rest[:, None]).astype(
                jnp.bfloat16
            )
            return 0

        def add(t, _):
            acc = None
            for n, (r, base) in enumerate(parts):
                term = r[base + t, :ROWS, :].astype(jnp.float32) * w_ref[n, pl.ds(t, 1), :]
                acc = term if acc is None else acc + term
            o_ref[t, :ROWS, :] = acc.astype(jnp.bfloat16)
            return 0

        lax.fori_loop(0, count // 8, note, 0, unroll=2)
        lax.fori_loop(0, count, add, 0, unroll=4)

    for h in range(2):
        parts, at = [], 0
        for cut in cuts:
            parts.append((refs[at], h * count) if cut == 1 else (refs[at + h], 0))
            at += cut
        pl.when(pl.program_id(0) == h)(functools.partial(join, parts))


def merged(parts):
    cuts = [len(p) for p in parts]
    arrays = [array for p in parts for array in p]
    rows = ROWS + META
    total = sum(array.shape[0] for array in parts[0])
    vmem = pl.BlockSpec(memory_space=pltpu.VMEM)
    return pl.pallas_call(
        functools.partial(merge_kernel, cuts),
        grid=(2,),
        in_specs=[vmem] * len(arrays),
        out_specs=pl.BlockSpec((total // 2, rows, HD), lambda i: (i, 0, 0)),
        scratch_shapes=[pltpu.VMEM((len(parts), total // 2, HD), jnp.float32)],
        out_shape=jax.ShapeDtypeStruct((total, rows, HD), jnp.bfloat16),
        compiler_params=pltpu.CompilerParams(
            dimension_semantics=("arbitrary",), vmem_limit_bytes=52 << 20
        ),
        cost_estimate=pl.CostEstimate(
            flops=8 * total * rows * HD,
            bytes_accessed=10 * total * rows * HD,
            transcendentals=0,
        ),
    )(*arrays)


def combine_kernel(holders, x_ref, own_ref, value_ref, o_ref, w_ref):
    users = value_ref.shape[0]
    low = lax.broadcasted_iota(jnp.int32, (1, HD), 1) < ROWS
    for u in range(users):
        own = own_ref[u]
        senders = [i for i, w in enumerate(holders) if w == u]
        pairs = [stats_of(x_ref[i, ROWS:, :].astype(jnp.float32), low) for i in senders]
        peak = own
        for top, _ in pairs:
            peak = jnp.maximum(peak, top)
        fresh = jnp.exp2(own - peak)
        total = fresh
        for i, (top, mass) in zip(senders, pairs):
            weight = mass * jnp.exp2(top - peak)
            w_ref[i : i + 1, :] = weight
            total = total + weight
        inverse = 1.0 / total
        acc = value_ref[u] * fresh
        for i in senders:
            acc = acc + x_ref[i, :ROWS, :].astype(jnp.float32) * w_ref[i : i + 1, :]
        turned = (acc * inverse).T
        o_ref[u] = jnp.concatenate([turned[:ROWS], turned[ROWS:]], axis=1).astype(
            jnp.bfloat16
        )


def combined(holders, x, own, value):
    users = value.shape[0]
    return pl.pallas_call(
        functools.partial(combine_kernel, holders),
        out_shape=jax.ShapeDtypeStruct((users, ROWS, HD), jnp.bfloat16),
        scratch_shapes=[pltpu.VMEM((x.shape[0], HD), jnp.float32)],
        compiler_params=pltpu.CompilerParams(vmem_limit_bytes=24 << 20),
        cost_estimate=pl.CostEstimate(
            flops=2 * x.size, bytes_accessed=2 * x.size, transcendentals=0
        ),
    )(x, own, value)


def moved(array, axis, step):
    if axis == "z":
        at = [(z % 2) * 2 + z // 2 for z in range(4)]
        pairs = [(at[z], at[(z + step) % 4]) for z in range(4)]
        return lax.ppermute(array, ("zl", "zh"), pairs)
    count = SIZES[FINE.index(axis)]
    return lax.ppermute(array, axis, [(i, (i + step) % count) for i in range(count)])


def body(queries, key_cache, value_cache, key_table, value_table, lengths, token_ids):
    users, beams, _ = queries.shape
    half = users // 2
    length = key_cache.shape[1]
    x, y, zl, zh, c = (lax.axis_index(n) for n in ("x", "y", "zl", "zh", "c"))
    row = (zl * SIZES[1] + y) * 2 + c
    col = x * SIZES[4] + zh
    swap = functools.partial(lax.ppermute, axis_name="c", perm=[(0, 1), (1, 0)])

    def halves(array):
        return (
            lax.dynamic_slice_in_dim(array, c * half, half, 0),
            lax.dynamic_slice_in_dim(array, (1 - c) * half, half, 0),
        )

    q = queries.reshape(users, beams, GROUP, HD).transpose(0, 2, 1, 3)
    q_mine, q_give = halves(q)
    t_mine, t_give = halves(token_ids)
    q_give, t_give, key_source = lax.optimization_barrier((q_give, t_give, key_cache))
    q_chip = jnp.concatenate([q_mine, swap(q_give)], axis=2).reshape(half, ROWS, HD)
    tokens = jnp.concatenate([t_mine, swap(t_give)], axis=1)

    holders = [
        (a + b + 2 * h + l) % half
        for l in range(SIZES[0])
        for b in range(SIZES[1])
        for a in range(SIZES[3])
        for h in range(SIZES[4])
    ]
    chips = len(holders)
    held = (x + y + 2 * zh + zl) % half
    marks = np.asarray(holders).reshape(chips, 1, 1)
    operand = jnp.broadcast_to(q_chip[0], (chips, ROWS, HD))
    for w in range(1, half):
        operand = jnp.where(marks == w, q_chip[w], operand)
    operand, value_source = lax.optimization_barrier((operand, value_cache))
    got = lax.all_to_all(operand, CHIPS, 0, 0, tiled=True)
    got = got.reshape(chips // KH, KH, ROWS, HD)

    k_other = swap(halves(key_source)[1])
    v_other = swap(halves(value_source)[1])
    got, k_other, v_other = lax.optimization_barrier((got, k_other, v_other))

    offset = (row * KH + col) * length
    other = ((row + 1 - 2 * c) * KH + col) * length

    info = jnp.stack([c * half, held, offset, other]).astype(jnp.int32)

    caches = (key_cache, k_other, value_cache, v_other)
    lead = got.shape[0] // 2
    computed = functools.partial(partials, info=info, lengths=lengths, caches=caches)

    def flat(parts):
        return [p.reshape(-1, ROWS + META, HD) for p in parts]

    ask1 = [moved(got[:lead], "x", 1), moved(got[lead:], "y", 1)]
    ask3 = [moved(got[:lead], "x", -1), moved(got[lead:], "y", -1)]
    ask2 = [moved(got, "z", 2)]
    begun = computed(0, asked=[got], parts=(0, PARTS // 2))
    ask1, ask3, begun = lax.optimization_barrier((ask1, ask3, begun))
    near, far = flat(computed(1, asked=ask1, results=2))
    back = [[moved(near, "x", -1), moved(far, "y", -1)]]
    ask3, _ = lax.optimization_barrier((ask3, near))
    near, far = flat(computed(-1, asked=ask3, results=2))
    back.append([moved(near, "x", 1), moved(far, "y", 1)])
    ask2, _, back[0] = lax.optimization_barrier((ask2, near, back[0]))
    near, far = flat(computed(2, asked=ask2, results=2))
    back.append([moved(near, "x", -2), moved(far, "z", -2)])
    begun, _ = lax.optimization_barrier((begun, near))
    back.append(
        flat(computed(0, asked=[got], parts=(PARTS // 2, PARTS - PARTS // 2), into=begun))
    )
    arrived = lax.all_to_all(merged(back), CHIPS, 0, 0, tiled=True)

    codes = jnp.arange(key_table.shape[0], dtype=jnp.int32)
    onehot = (tokens[..., None] == codes).astype(jnp.bfloat16)
    keys = lax.dynamic_slice_in_dim(key_table, col * HD, HD, 1)
    values = lax.dynamic_slice_in_dim(value_table, col * HD, HD, 1)
    own_keys = jnp.einsum("uwv,vc->uwc", onehot, keys, preferred_element_type=jnp.float32)
    own_values = jnp.einsum("uwv,vc->uwc", onehot, values, preferred_element_type=jnp.float32)
    q_rows = q_chip.reshape(half, GROUP, 2 * beams, HD).astype(jnp.float32)
    own = jnp.sum(q_rows * own_keys[:, None], axis=-1) * SCALE2
    own = jnp.tile(own.reshape(half, 1, ROWS), (1, 1, 2))
    own_values = own_values.reshape(half, 2 * beams, 2, HALF).transpose(0, 3, 2, 1)
    own_values = jnp.broadcast_to(
        own_values[:, :, :, None], (half, HALF, 2, GROUP, 2 * beams)
    ).reshape(half, HALF, HD)

    result = combined(holders, arrived, own, own_values)
    result = result.reshape(half, GROUP, 2 * beams, HD)
    kept = result[:, :, :beams]
    received = swap(result[:, :, beams:])
    whole = jnp.where(
        c == 0, jnp.concatenate([kept, received]), jnp.concatenate([received, kept])
    )
    return whole.transpose(0, 2, 1, 3).reshape(users, beams, GROUP * HD)


def solution(mesh):
    fine = Mesh(np.asarray(mesh.devices).reshape(SIZES), FINE)
    row, col = ("zl", "y", "c"), ("x", "zh")
    return jax.shard_map(
        body,
        mesh=fine,
        in_specs=(
            P(None, row, col),
            P(None, row + col, None),
            P(None, row + col, None),
            P(),
            P(),
            P(),
            P(None, row),
        ),
        out_specs=P(None, row, col),
        check_vma=False,
    )
```

profile of v0, /device:TPU:1, one launch (start us, length us, event | category | flops | bytes accessed | tf_op | source)
XLA Modules:
  0.0 146.0 jit_solution(10909749949591957638)
XLA Ops:
  0.0 0.9 dynamic-slice_bitcast_fusion
  1.7 1.5 %collective-permute-start = (bf16[4,4,8,128]{3,2,1,0:T(8,128)(2,1)S(1)}, bf16[4,4,8,128]{3,2,1,0:T(8,128)(2,1)S(1)}, u32[]{:S(2)}, u32[]{:S(2)}) collective-permute-start(bf16[4,4,8,128]{3,2,1,0:T(8,128)(2,1)S(1)} %get-tuple-element.30), channel_id=1, source_target_pairs={{0,8},{8,0},{1,9},{9,1},{2,10},{10,2},{3,11},{11,3},{4,12},{12,4},... | collective-permute-start | bytes 98312 | tf_op jit(solution)/shard_map/ppermute | solution.py:317
  3.2 3.3 %constant_dynamic-slice_fusion.2 = bf16[4,512,1024]{2,1,0:T(8,128)(2,1)S(1)} fusion(bf16[8,512,1024]{2,1,0:T(8,128)(2,1)} %refs_1_.5, s32[]{:T(128)S(6)} %select_n.41), kind=kLoop, calls=%fused_computation.34 | loop fusion | bytes 8388612 | tf_op jit(solution)/shard_map/dynamic_slice | solution.py:310
  8.3 28.6 %all_to_all.10 = bf16[64,64,128]{2,1,0:T(8,128)(2,1)} all-to-all(bf16[64,64,128]{2,1,0:T(8,128)(2,1)S(1)} %select_select_fusion), channel_id=1, replica_groups=mesh['zl'=2,'y'=4,'c'=2,'x'=4,'zh'=2] {'zl','y','x','zh'}, dimensions={0} | all-to-all | bytes 2097152 | tf_op jit(solution)/shard_map/all_to_all | solution.py:334
  37.0 2.2 %fusion.15 = (bf16[4,8,64,128]{3,2,1,0:T(8,128)(2,1)}, bf16[4,8,64,128]{3,2,1,0:T(8,128)(2,1)}) fusion(bf16[8,8,64,128]{3,2,1,0:T(8,128)(2,1)} %bitcast.7.refs_0_), kind=kLoop, calls=%fused_computation.37 | loop fusion | bytes 2097152 | tf_op jit(solution)/shard_map/slice | solution.py:353
  40.2 2.2 %collective-permute-start.6 = (bf16[4,8,64,128]{3,2,1,0:T(8,128)(2,1)}, bf16[4,8,64,128]{3,2,1,0:T(8,128)(2,1)S(1)}, u32[]{:S(2)}, u32[]{:S(2)}) collective-permute-start(bf16[4,8,64,128]{3,2,1,0:T(8,128)(2,1)} %get-tuple-element.56), channel_id=1, source_target_pairs={{0,6},{2,0},{4,2},{6,4},{1,7},{3,1},{5,3},{7,5},{8,14},{10,8},{12,... | collective-permute-start | bytes 1572872 | tf_op jit(solution)/shard_map/ppermute | solution.py:295
  42.4 2.2 %collective-permute-start.7 = (bf16[4,8,64,128]{3,2,1,0:T(8,128)(2,1)}, bf16[4,8,64,128]{3,2,1,0:T(8,128)(2,1)S(1)}, u32[]{:S(2)}, u32[]{:S(2)}) collective-permute-start(bf16[4,8,64,128]{3,2,1,0:T(8,128)(2,1)} %get-tuple-element.55), channel_id=1, source_target_pairs={{0,48},{16,0},{32,16},{48,32},{1,49},{17,1},{33,17},{49,33},{2,50}... | collective-permute-start | bytes 1572872 | tf_op jit(solution)/shard_map/ppermute | solution.py:295
  44.6 1.0 collective-permute-start.3
  46.2 6.7 %shard_map.100.refs_5_ = bf16[8,8,72,128]{3,2,1,0:T(8,128)(2,1)} custom-call(s32[4]{0:T(128)} %pad_add_fusion.1.info, s32[8]{0:T(128)} %lengths.9, bf16[8,8,64,128]{3,2,1,0:T(8,128)(2,1)} %bitcast.7.refs_0_, bf16[8,512,1024]{2,1,0:T(8,128)(2,1)} %refs_1_.5, bf16[4,512,1024]{2,1,0:T(8,128)(2,1)} %collective-permute-done.1.refs_2_.refs_3_, ...), custom_call_target="tpu_custom_call" | custom-call | flops 1073741824 | bytes 2097152 | tf_op jit(solution)/shard_map/pallas_call | solution.py:147
  53.6 9.9 %shard_map.101 = (bf16[4,8,72,128]{3,2,1,0:T(8,128)(2,1)}, bf16[4,8,72,128]{3,2,1,0:T(8,128)(2,1)}) custom-call(s32[4]{0:T(128)} %pad_add_fusion.1.info, s32[8]{0:T(128)} %lengths.9, bf16[4,8,64,128]{3,2,1,0:T(8,128)(2,1)} %collective-permute-done.4.refs_0_, bf16[4,8,64,128]{3,2,1,0:T(8,128)(2,1)} %collective-permute-done.5.refs_1_, ...), custom_call_target="tpu_custom_call" | custom-call | flops 2147483648 | bytes 4194304 | tf_op jit(solution)/shard_map/pallas_call | solution.py:147
  63.4 1.6 %collective-permute-start.8 = (bf16[32,72,128]{2,1,0:T(8,128)(2,1)}, bf16[32,72,128]{2,1,0:T(8,128)(2,1)S(1)}, u32[]{:S(2)}, u32[]{:S(2)}) collective-permute-start(bf16[32,72,128]{2,1,0:T(8,128)(2,1)} %bitcast.46), channel_id=1, source_target_pairs={{0,6},{2,0},{4,2},{6,4},{1,7},{3,1},{5,3},{7,5},{8,14},{10,8},{12,... | collective-permute-start | bytes 1769480 | tf_op jit(solution)/shard_map/ppermute | solution.py:295
  65.1 3.4 %collective-permute-start.9 = (bf16[32,72,128]{2,1,0:T(8,128)(2,1)}, bf16[32,72,128]{2,1,0:T(8,128)(2,1)S(1)}, u32[]{:S(2)}, u32[]{:S(2)}) collective-permute-start(bf16[32,72,128]{2,1,0:T(8,128)(2,1)} %bitcast.45), channel_id=1, source_target_pairs={{0,48},{16,0},{32,16},{48,32},{1,49},{17,1},{33,17},{49,33},{2,50}... | collective-permute-start | bytes 1769480 | tf_op jit(solution)/shard_map/ppermute | solution.py:295
  68.5 9.9 %shard_map.102 = (bf16[4,8,72,128]{3,2,1,0:T(8,128)(2,1)}, bf16[4,8,72,128]{3,2,1,0:T(8,128)(2,1)}) custom-call(s32[4]{0:T(128)} %pad_add_fusion.1.info, s32[8]{0:T(128)} %lengths.9, bf16[4,8,64,128]{3,2,1,0:T(8,128)(2,1)} %copy-done.3, bf16[4,8,64,128]{3,2,1,0:T(8,128)(2,1)} %copy-done.4, bf16[8,512,1024]{2,1,0:T(8,128)(2,1)} %refs_1_.5, ...), custom_call_target="tpu_custom_call" | custom-call | flops 2147483648 | bytes 4194304 | tf_op jit(solution)/shard_map/pallas_call | solution.py:147
  79.5 9.8 %shard_map.103 = (bf16[4,8,72,128]{3,2,1,0:T(8,128)(2,1)}, bf16[4,8,72,128]{3,2,1,0:T(8,128)(2,1)}) custom-call(s32[4]{0:T(128)} %pad_add_fusion.1.info, s32[8]{0:T(128)} %lengths.9, bf16[8,8,64,128]{3,2,1,0:T(8,128)(2,1)} %collective-permute-done.3.refs_0_, bf16[8,512,1024]{2,1,0:T(8,128)(2,1)} %refs_1_.5, ...), custom_call_target="tpu_custom_call" | custom-call | flops 2147483648 | bytes 4194304 | tf_op jit(solution)/shard_map/pallas_call | solution.py:147
  89.4 3.0 %collective-permute-start.12 = (bf16[32,72,128]{2,1,0:T(8,128)(2,1)}, bf16[32,72,128]{2,1,0:T(8,128)(2,1)}, u32[]{:S(2)}, u32[]{:S(2)}) collective-permute-start(bf16[32,72,128]{2,1,0:T(8,128)(2,1)} %bitcast.48), channel_id=1, source_target_pairs={{0,4},{2,6},{4,0},{6,2},{1,5},{3,7},{5,1},{7,3},{8,12},{10,14},{12... | collective-permute-start | bytes 1769480 | tf_op jit(solution)/shard_map/ppermute | solution.py:295
  92.4 6.5 %shard_map.104 = bf16[8,8,72,128]{3,2,1,0:T(8,128)(2,1)} custom-call(s32[4]{0:T(128)} %pad_add_fusion.1.info, s32[8]{0:T(128)} %lengths.9, bf16[8,8,64,128]{3,2,1,0:T(8,128)(2,1)} %bitcast.7.refs_0_, bf16[8,512,1024]{2,1,0:T(8,128)(2,1)} %refs_1_.5, bf16[4,512,1024]{2,1,0:T(8,128)(2,1)} %collective-permute-done.1.refs_2_.refs_3_, ...), custom_call_target="tpu_custom_call", output_to_operand_aliasing={{}: (7, {})} | custom-call | flops 1073741824 | bytes 2097152 | tf_op jit(solution)/shard_map/pallas_call | solution.py:147
  98.9 8.4 %collective-permute-done.12.refs_4_ = bf16[32,72,128]{2,1,0:T(8,128)(2,1)} collective-permute-done((bf16[32,72,128]{2,1,0:T(8,128)(2,1)}, bf16[32,72,128]{2,1,0:T(8,128)(2,1)}, u32[]{:S(2)}, u32[]{:S(2)}) %collective-permute-start.12) | collective-permute-done | bytes 589856 | tf_op jit(solution)/shard_map/ppermute | solution.py:295
  107.3 4.3 %shard_map.105 = bf16[64,72,128]{2,1,0:T(8,128)(2,1)} custom-call(bf16[32,72,128]{2,1,0:T(8,128)(2,1)S(1)} %collective-permute-done.8.refs_0_, bf16[32,72,128]{2,1,0:T(8,128)(2,1)S(1)} %collective-permute-done.9.refs_1_, bf16[32,72,128]{2,1,0:T(8,128)(2,1)} %collective-permute-done.10.refs_2_, bf16[32,72,128]{2,1,0:T(8,128)(2,1)} %copy-done.2, ...), custom_call_target="tpu_custom_call" | custom-call | flops 4718592 | bytes 5898240 | tf_op jit(solution)/shard_map/pallas_call | solution.py:232
  111.6 11.6 %all-to-all-start.1 = ((bf16[64,72,128]{2,1,0:T(8,128)(2,1)}), bf16[64,72,128]{2,1,0:T(8,128)(2,1)S(1)}, u32[]{:S(2)}, u32[]{:S(2)}) async-start(bf16[64,72,128]{2,1,0:T(8,128)(2,1)} %shard_map.105), calls=%async_computation.1 | async-start | bytes 2359296 | tf_op jit(solution)/shard_map/all_to_all | solution.py:370
  123.2 1.6 %collective-permute-start.14 = (s32[4,8]{1,0:T(4,128)S(1)}, s32[4,8]{1,0:T(4,128)S(1)}, u32[]{:S(2)}, u32[]{:S(2)}) collective-permute-start(s32[4,8]{1,0:T(4,128)S(1)} %get-tuple-element.54), channel_id=1, source_target_pairs={{0,8},{8,0},{1,9},{9,1},{2,10},{10,2},{3,11},{11,3},{4,12},{12,4},... | collective-permute-start | bytes 392 | tf_op jit(solution)/shard_map/ppermute | solution.py:318
  126.8 1.1 copy.14.value_ref
  127.9 1.2 fusion.2
  129.4 11.0 %all-to-all-done.1.x_ref = bf16[64,72,128]{2,1,0:T(8,128)(2,1)S(1)} async-done(((bf16[64,72,128]{2,1,0:T(8,128)(2,1)}), bf16[64,72,128]{2,1,0:T(8,128)(2,1)S(1)}, u32[]{:S(2)}, u32[]{:S(2)}) %all-to-all-start.1) | async-done | bytes 1179680 | tf_op jit(solution)/shard_map/all_to_all | solution.py:370
  141.0 3.6 %collective-permute-start.15 = (bf16[4,4,8,128]{3,2,1,0:T(8,128)(2,1)S(1)}, bf16[4,4,8,128]{3,2,1,0:T(8,128)(2,1)S(1)}, u32[]{:S(2)}, u32[]{:S(2)}) collective-permute-start(bf16[4,4,8,128]{3,2,1,0:T(8,128)(2,1)S(1)} %get-tuple-element.58), channel_id=1, source_target_pairs={{0,8},{8,0},{1,9},{9,1},{2,10},{10,2},{3,11},{11,3},{4,12},{12,4},... | collective-permute-start | bytes 98312 | tf_op jit(solution)/shard_map/ppermute | solution.py:389
  (56 shorter events, 10.3 us)
Async XLA Ops:
  0.0 125.7 %copy-start = (bf16[1024,1024]{1,0:T(8,128)(2,1)S(1)}, bf16[1024,1024]{1,0:T(8,128)(2,1)}, u32[]{:S(2)}) copy-start(bf16[1024,1024]{1,0:T(8,128)(2,1)} %param.14) | copy-start | bytes 6291460
  1.7 4.9 %copy-start.6 = (pred[64]{0:T(512)(128)(4,1)S(1)}, pred[64]{0:T(512)(128)(4,1)}, u32[]{:S(2)}) copy-start(pred[64]{0:T(512)(128)(4,1)} %constant.61) | copy-start | bytes 196
  1.7 5.0 %copy-start.7 = (pred[64]{0:T(512)(128)(4,1)S(1)}, pred[64]{0:T(512)(128)(4,1)}, u32[]{:S(2)}) copy-start(pred[64]{0:T(512)(128)(4,1)} %constant.62) | copy-start | bytes 196
  1.7 5.2 %copy-start.1 = (bf16[8,512,1024]{2,1,0:T(8,128)(2,1)S(1)}, bf16[8,512,1024]{2,1,0:T(8,128)(2,1)}, u32[]{:S(2)}) copy-start(bf16[8,512,1024]{2,1,0:T(8,128)(2,1)} %refs_3_.5) | copy-start | bytes 25165828
  1.7 4.9 %collective-permute-start = (bf16[4,4,8,128]{3,2,1,0:T(8,128)(2,1)S(1)}, bf16[4,4,8,128]{3,2,1,0:T(8,128)(2,1)S(1)}, u32[]{:S(2)}, u32[]{:S(2)}) collective-permute-start(bf16[4,4,8,128]{3,2,1,0:T(8,128)(2,1)S(1)} %get-tuple-element.30), channel_id=1, source_target_pairs={{0,8},{8,0},{1,9},{9,1},{2,10},{10,2},{3,11},{11,3},{4,12},{12,4},... | collective-permute-start | bytes 98312 | tf_op jit(solution)/shard_map/ppermute | solution.py:317
  6.5 30.5 %collective-permute-start.1 = (bf16[4,512,1024]{2,1,0:T(8,128)(2,1)S(1)}, bf16[4,512,1024]{2,1,0:T(8,128)(2,1)}, u32[]{:S(2)}, u32[]{:S(2)}) collective-permute-start(bf16[4,512,1024]{2,1,0:T(8,128)(2,1)S(1)} %constant_dynamic-slice_fusion.2), channel_id=1, source_target_pairs={{0,8},{8,0},{1,9},{9,1},{2,10},{10,2},{3,11},{11,3},{4,12},{12,4},... | collective-permute-start | bytes 12582920 | tf_op jit(solution)/shard_map/ppermute | solution.py:337
  7.4 29.6 %collective-permute-start.2 = (bf16[4,512,1024]{2,1,0:T(8,128)(2,1)S(1)}, bf16[4,512,1024]{2,1,0:T(8,128)(2,1)}, u32[]{:S(2)}, u32[]{:S(2)}) collective-permute-start(bf16[4,512,1024]{2,1,0:T(8,128)(2,1)S(1)} %constant_dynamic-slice_fusion.1), channel_id=1, source_target_pairs={{0,8},{8,0},{1,9},{9,1},{2,10},{10,2},{3,11},{11,3},{4,12},{12,4},... | collective-permute-start | bytes 12582920 | tf_op jit(solution)/shard_map/ppermute | solution.py:338
  39.2 13.7 %collective-permute-start.4 = (bf16[4,8,64,128]{3,2,1,0:T(8,128)(2,1)}, bf16[4,8,64,128]{3,2,1,0:T(8,128)(2,1)}, u32[]{:S(2)}, u32[]{:S(2)}) collective-permute-start(bf16[4,8,64,128]{3,2,1,0:T(8,128)(2,1)} %get-tuple-element.56), channel_id=1, source_target_pairs={{0,2},{2,4},{4,6},{6,0},{1,3},{3,5},{5,7},{7,1},{8,10},{10,12},{12... | collective-permute-start | bytes 1572872 | tf_op jit(solution)/shard_map/ppermute | solution.py:295
  39.8 13.1 %collective-permute-start.5 = (bf16[4,8,64,128]{3,2,1,0:T(8,128)(2,1)}, bf16[4,8,64,128]{3,2,1,0:T(8,128)(2,1)}, u32[]{:S(2)}, u32[]{:S(2)}) collective-permute-start(bf16[4,8,64,128]{3,2,1,0:T(8,128)(2,1)} %get-tuple-element.55), channel_id=1, source_target_pairs={{0,16},{16,32},{32,48},{48,0},{1,17},{17,33},{33,49},{49,1},{2,18}... | collective-permute-start | bytes 1572872 | tf_op jit(solution)/shard_map/ppermute | solution.py:295
  40.2 12.7 %collective-permute-start.6 = (bf16[4,8,64,128]{3,2,1,0:T(8,128)(2,1)}, bf16[4,8,64,128]{3,2,1,0:T(8,128)(2,1)S(1)}, u32[]{:S(2)}, u32[]{:S(2)}) collective-permute-start(bf16[4,8,64,128]{3,2,1,0:T(8,128)(2,1)} %get-tuple-element.56), channel_id=1, source_target_pairs={{0,6},{2,0},{4,2},{6,4},{1,7},{3,1},{5,3},{7,5},{8,14},{10,8},{12,... | collective-permute-start | bytes 1572872 | tf_op jit(solution)/shard_map/ppermute | solution.py:295
  42.4 11.2 %collective-permute-start.7 = (bf16[4,8,64,128]{3,2,1,0:T(8,128)(2,1)}, bf16[4,8,64,128]{3,2,1,0:T(8,128)(2,1)S(1)}, u32[]{:S(2)}, u32[]{:S(2)}) collective-permute-start(bf16[4,8,64,128]{3,2,1,0:T(8,128)(2,1)} %get-tuple-element.55), channel_id=1, source_target_pairs={{0,48},{16,0},{32,16},{48,32},{1,49},{17,1},{33,17},{49,33},{2,50}... | collective-permute-start | bytes 1572872 | tf_op jit(solution)/shard_map/ppermute | solution.py:295
  44.6 34.1 %collective-permute-start.3 = (bf16[8,8,64,128]{3,2,1,0:T(8,128)(2,1)}, bf16[8,8,64,128]{3,2,1,0:T(8,128)(2,1)}, u32[]{:S(2)}, u32[]{:S(2)}) collective-permute-start(bf16[8,8,64,128]{3,2,1,0:T(8,128)(2,1)} %bitcast.7.refs_0_), channel_id=1, source_target_pairs={{0,1},{64,65},{1,0},{65,64},{2,3},{66,67},{3,2},{67,66},{4,5},{68,... | collective-permute-start | bytes 3145736 | tf_op jit(solution)/shard_map/ppermute | solution.py:293
  52.9 10.5 %copy-start.3 = (bf16[4,8,64,128]{3,2,1,0:T(8,128)(2,1)}, bf16[4,8,64,128]{3,2,1,0:T(8,128)(2,1)S(1)}, u32[]{:S(2)}) copy-start(bf16[4,8,64,128]{3,2,1,0:T(8,128)(2,1)S(1)} %collective-permute-done.6.refs_0_) | copy-start | bytes 1572868
  53.6 9.9 %copy-start.4 = (bf16[4,8,64,128]{3,2,1,0:T(8,128)(2,1)}, bf16[4,8,64,128]{3,2,1,0:T(8,128)(2,1)S(1)}, u32[]{:S(2)}) copy-start(bf16[4,8,64,128]{3,2,1,0:T(8,128)(2,1)S(1)} %collective-permute-done.7.refs_1_) | copy-start | bytes 1572868
  63.4 15.3 %collective-permute-start.8 = (bf16[32,72,128]{2,1,0:T(8,128)(2,1)}, bf16[32,72,128]{2,1,0:T(8,128)(2,1)S(1)}, u32[]{:S(2)}, u32[]{:S(2)}) collective-permute-start(bf16[32,72,128]{2,1,0:T(8,128)(2,1)} %bitcast.46), channel_id=1, source_target_pairs={{0,6},{2,0},{4,2},{6,4},{1,7},{3,1},{5,3},{7,5},{8,14},{10,8},{12,... | collective-permute-start | bytes 1769480 | tf_op jit(solution)/shard_map/ppermute | solution.py:295
  65.1 14.5 %collective-permute-start.9 = (bf16[32,72,128]{2,1,0:T(8,128)(2,1)}, bf16[32,72,128]{2,1,0:T(8,128)(2,1)S(1)}, u32[]{:S(2)}, u32[]{:S(2)}) collective-permute-start(bf16[32,72,128]{2,1,0:T(8,128)(2,1)} %bitcast.45), channel_id=1, source_target_pairs={{0,48},{16,0},{32,16},{48,32},{1,49},{17,1},{33,17},{49,33},{2,50}... | collective-permute-start | bytes 1769480 | tf_op jit(solution)/shard_map/ppermute | solution.py:295
  78.4 20.5 %collective-permute-start.10 = (bf16[32,72,128]{2,1,0:T(8,128)(2,1)}, bf16[32,72,128]{2,1,0:T(8,128)(2,1)}, u32[]{:S(2)}, u32[]{:S(2)}) collective-permute-start(bf16[32,72,128]{2,1,0:T(8,128)(2,1)} %bitcast.44), channel_id=1, source_target_pairs={{0,2},{2,4},{4,6},{6,0},{1,3},{3,5},{5,7},{7,1},{8,10},{10,12},{12... | collective-permute-start | bytes 1769480 | tf_op jit(solution)/shard_map/ppermute | solution.py:295
  78.4 20.5 %collective-permute-start.11 = (bf16[32,72,128]{2,1,0:T(8,128)(2,1)}, bf16[32,72,128]{2,1,0:T(8,128)(2,1)S(1)}, u32[]{:S(2)}, u32[]{:S(2)}) collective-permute-start(bf16[32,72,128]{2,1,0:T(8,128)(2,1)} %bitcast.43), channel_id=1, source_target_pairs={{0,16},{16,32},{32,48},{48,0},{1,17},{17,33},{33,49},{49,1},{2,18}... | collective-permute-start | bytes 1769480 | tf_op jit(solution)/shard_map/ppermute | solution.py:295
  89.4 17.9 %collective-permute-start.12 = (bf16[32,72,128]{2,1,0:T(8,128)(2,1)}, bf16[32,72,128]{2,1,0:T(8,128)(2,1)}, u32[]{:S(2)}, u32[]{:S(2)}) collective-permute-start(bf16[32,72,128]{2,1,0:T(8,128)(2,1)} %bitcast.48), channel_id=1, source_target_pairs={{0,4},{2,6},{4,0},{6,2},{1,5},{3,7},{5,1},{7,3},{8,12},{10,14},{12... | collective-permute-start | bytes 1769480 | tf_op jit(solution)/shard_map/ppermute | solution.py:295
  92.4 14.9 %collective-permute-start.13 = (bf16[32,72,128]{2,1,0:T(8,128)(2,1)}, bf16[32,72,128]{2,1,0:T(8,128)(2,1)}, u32[]{:S(2)}, u32[]{:S(2)}) collective-permute-start(bf16[32,72,128]{2,1,0:T(8,128)(2,1)} %bitcast.47), channel_id=1, source_target_pairs={{0,1},{64,65},{1,0},{65,64},{2,3},{66,67},{3,2},{67,66},{4,5},{68,... | collective-permute-start | bytes 1769480 | tf_op jit(solution)/shard_map/ppermute | solution.py:293
  98.9 8.4 %copy-start.2 = (bf16[32,72,128]{2,1,0:T(8,128)(2,1)}, bf16[32,72,128]{2,1,0:T(8,128)(2,1)S(1)}, u32[]{:S(2)}) copy-start(bf16[32,72,128]{2,1,0:T(8,128)(2,1)S(1)} %collective-permute-done.11.refs_3_) | copy-start | bytes 1769476
  111.6 28.8 %all-to-all-start.1 = ((bf16[64,72,128]{2,1,0:T(8,128)(2,1)}), bf16[64,72,128]{2,1,0:T(8,128)(2,1)S(1)}, u32[]{:S(2)}, u32[]{:S(2)}) async-start(bf16[64,72,128]{2,1,0:T(8,128)(2,1)} %shard_map.105), calls=%async_computation.1 | async-start | bytes 2359296 | tf_op jit(solution)/shard_map/all_to_all | solution.py:370
  123.2 2.4 %collective-permute-start.14 = (s32[4,8]{1,0:T(4,128)S(1)}, s32[4,8]{1,0:T(4,128)S(1)}, u32[]{:S(2)}, u32[]{:S(2)}) collective-permute-start(s32[4,8]{1,0:T(4,128)S(1)} %get-tuple-element.54), channel_id=1, source_target_pairs={{0,8},{8,0},{1,9},{9,1},{2,10},{10,2},{3,11},{11,3},{4,12},{12,4},... | collective-permute-start | bytes 392 | tf_op jit(solution)/shard_map/ppermute | solution.py:318
  141.0 4.5 %collective-permute-start.15 = (bf16[4,4,8,128]{3,2,1,0:T(8,128)(2,1)S(1)}, bf16[4,4,8,128]{3,2,1,0:T(8,128)(2,1)S(1)}, u32[]{:S(2)}, u32[]{:S(2)}) collective-permute-start(bf16[4,4,8,128]{3,2,1,0:T(8,128)(2,1)S(1)} %get-tuple-element.58), channel_id=1, source_target_pairs={{0,8},{8,0},{1,9},{9,1},{2,10},{10,2},{3,11},{11,3},{4,12},{12,4},... | collective-permute-start | bytes 98312 | tf_op jit(solution)/shard_map/ppermute | solution.py:389
  (1 other events, 4.9 us)
where the time goes:
time: 145 us; the launch traced here: 146 us
  Pallas kernels  47.6 us (33%)
  starting transfers between devices  34 us (23%)
  blocking collectives  28.6 us (20%)
  waiting for transfers between devices  22.6 us (16%)
  local copies, waits for them, and re-layouts  9.77 us (7%)
  other arithmetic  1.76 us (1%)
    pallas_call x5, Pallas kernels, partials(): pl.pallas_call(functools.partial(partial_kernel, step, len(asked), result...  42.8 us
    all_to_all x1, blocking collectives, body(): got = lax.all_to_all(operand, CHIPS, 0, 0, tiled=True)  28.6 us
    ppermute x9, starting transfers between devices, moved(): lax.ppermute(array, axis, [(i, (i + step) % count) for i in range(count)])  13.7 us
    all_to_all x1, starting transfers between devices, body(): arrived = lax.all_to_all(merged(back), CHIPS, 0, 0, tiled=True)  11.6 us
    all_to_all x1, waiting for transfers between devices, body(): arrived = lax.all_to_all(merged(back), CHIPS, 0, 0, tiled=True)  11 us
    ppermute x9, waiting for transfers between devices, moved(): lax.ppermute(array, axis, [(i, (i + step) % count) for i in range(count)])  9.88 us
    dynamic_slice x3, local copies, waits for them, and re-layouts, halves(): lax.dynamic_slice_in_dim(array, (1 - c) * half, half, 0)  4.67 us
    pallas_call x1, Pallas kernels, merged(): pl.pallas_call(functools.partial(merge_kernel, cuts), grid=(2,), in_specs...  4.3 us
  transfers between devices with their start and end apart: 17, of which 6 were waited for; matrix products, arithmetic and copies ran while one was open for 6% of the time, Pallas kernels for 29%

commit v1 on v0

--- a/solution.py
+++ b/solution.py
@@ -212,8 +212,8 @@
             o_ref[t, :ROWS, :] = acc.astype(jnp.bfloat16)
             return 0
 
-        lax.fori_loop(0, count // 8, note, 0, unroll=2)
-        lax.fori_loop(0, count, add, 0, unroll=4)
+        lax.fori_loop(0, count // 8, note, 0, unroll=4)
+        lax.fori_loop(0, count, add, 0, unroll=8)
 
     for h in range(2):
         parts, at = [], 0
@@ -313,7 +313,7 @@
     q = queries.reshape(users, beams, GROUP, HD).transpose(0, 2, 1, 3)
     q_mine, q_give = halves(q)
     t_mine, t_give = halves(token_ids)
-    q_give, t_give, key_source = lax.optimization_barrier((q_give, t_give, key_cache))
+    q_give, key_source = lax.optimization_barrier((q_give, key_cache))
     q_chip = jnp.concatenate([q_mine, swap(q_give)], axis=2).reshape(half, ROWS, HD)
     tokens = jnp.concatenate([t_mine, swap(t_give)], axis=1)
 

time: 145 us -> 141 us (0.972); the launches traced: 146 us -> 140 us
  waiting for transfers between devices: 22.6 us -> 19.9 us
  starting transfers between devices: 34 us -> 31.5 us
    ppermute x9, waiting for transfers between devices: 9.88 us -> 7.77 us  [moved(): lax.ppermute(array, axis, [(i, (i + step) % count) for i in range(count)])]
    ppermute x9, starting transfers between devices: 13.7 us -> 11.8 us  [moved(): lax.ppermute(array, axis, [(i, (i + step) % count) for i in range(count)])]
  transfers between devices with their start and end apart: 17 -> 17, of which waited for: 6 -> 5; matrix products, arithmetic and copies ran while one was open for 6% -> 6% of each run, Pallas kernels for 29% -> 31%
where the time goes in v1:
time: 141 us; the launch traced here: 140 us
  Pallas kernels  47.4 us (34%)
  starting transfers between devices  31.5 us (22%)
  blocking collectives  28.6 us (20%)
  waiting for transfers between devices  19.9 us (14%)
  local copies, waits for them, and re-layouts  9.02 us (6%)
  other arithmetic  1.79 us (1%)
  matrix products  1.43 us (1%)
    pallas_call x5, Pallas kernels, partials(): pl.pallas_call(functools.partial(partial_kernel, step, len(asked), result...  42.7 us
    all_to_all x1, blocking collectives, body(): got = lax.all_to_all(operand, CHIPS, 0, 0, tiled=True)  28.6 us
    ppermute x9, starting transfers between devices, moved(): lax.ppermute(array, axis, [(i, (i + step) % count) for i in range(count)])  11.8 us
    all_to_all x1, starting transfers between devices, body(): arrived = lax.all_to_all(merged(back), CHIPS, 0, 0, tiled=True)  10.5 us
    all_to_all x1, waiting for transfers between devices, body(): arrived = lax.all_to_all(merged(back), CHIPS, 0, 0, tiled=True)  10.4 us
    ppermute x9, waiting for transfers between devices, moved(): lax.ppermute(array, axis, [(i, (i + step) % count) for i in range(count)])  7.77 us
    dynamic_slice x3, local copies, waits for them, and re-layouts, halves(): lax.dynamic_slice_in_dim(array, (1 - c) * half, half, 0)  4.66 us
    pallas_call x1, Pallas kernels, merged(): pl.pallas_call(functools.partial(merge_kernel, cuts), grid=(2,), in_specs...  4.08 us
  transfers between devices with their start and end apart: 17, of which 5 were waited for; matrix products, arithmetic and copies ran while one was open for 6% of the time, Pallas kernels for 31%

profile of v1, /device:TPU:1, one launch (start us, length us, event | category | flops | bytes accessed | tf_op | source)
XLA Modules:
  0.0 139.9 jit_solution(1864524609647647873)
XLA Ops:
  0.0 0.9 dynamic-slice_bitcast_fusion
  1.0 1.5 %collective-permute-start = (bf16[4,4,8,128]{3,2,1,0:T(8,128)(2,1)S(1)}, bf16[4,4,8,128]{3,2,1,0:T(8,128)(2,1)S(1)}, u32[]{:S(2)}, u32[]{:S(2)}) collective-permute-start(bf16[4,4,8,128]{3,2,1,0:T(8,128)(2,1)S(1)} %get-tuple-element.29), channel_id=1, source_target_pairs={{0,8},{8,0},{1,9},{9,1},{2,10},{10,2},{3,11},{11,3},{4,12},{12,4},... | collective-permute-start | bytes 98312 | tf_op jit(solution)/shard_map/ppermute | solution.py:317
  2.5 3.3 %constant_dynamic-slice_fusion.3 = bf16[4,512,1024]{2,1,0:T(8,128)(2,1)S(1)} fusion(bf16[8,512,1024]{2,1,0:T(8,128)(2,1)} %refs_1_.5, s32[]{:T(128)S(6)} %select_n.41), kind=kLoop, calls=%fused_computation.35 | loop fusion | bytes 8388612 | tf_op jit(solution)/shard_map/dynamic_slice | solution.py:310
  7.6 28.6 %all_to_all.10 = bf16[64,64,128]{2,1,0:T(8,128)(2,1)} all-to-all(bf16[64,64,128]{2,1,0:T(8,128)(2,1)S(1)} %select_select_fusion), channel_id=1, replica_groups=mesh['zl'=2,'y'=4,'c'=2,'x'=4,'zh'=2] {'zl','y','x','zh'}, dimensions={0} | all-to-all | bytes 2097152 | tf_op jit(solution)/shard_map/all_to_all | solution.py:334
  36.2 2.2 %fusion.15 = (bf16[4,8,64,128]{3,2,1,0:T(8,128)(2,1)}, bf16[4,8,64,128]{3,2,1,0:T(8,128)(2,1)}) fusion(bf16[8,8,64,128]{3,2,1,0:T(8,128)(2,1)} %bitcast.7.refs_0_), kind=kLoop, calls=%fused_computation.37 | loop fusion | bytes 2097152 | tf_op jit(solution)/shard_map/slice | solution.py:353
  39.5 2.2 %collective-permute-start.6 = (bf16[4,8,64,128]{3,2,1,0:T(8,128)(2,1)}, bf16[4,8,64,128]{3,2,1,0:T(8,128)(2,1)S(1)}, u32[]{:S(2)}, u32[]{:S(2)}) collective-permute-start(bf16[4,8,64,128]{3,2,1,0:T(8,128)(2,1)} %get-tuple-element.54), channel_id=1, source_target_pairs={{0,6},{2,0},{4,2},{6,4},{1,7},{3,1},{5,3},{7,5},{8,14},{10,8},{12,... | collective-permute-start | bytes 1572872 | tf_op jit(solution)/shard_map/ppermute | solution.py:295
  41.6 2.2 %collective-permute-start.7 = (bf16[4,8,64,128]{3,2,1,0:T(8,128)(2,1)}, bf16[4,8,64,128]{3,2,1,0:T(8,128)(2,1)S(1)}, u32[]{:S(2)}, u32[]{:S(2)}) collective-permute-start(bf16[4,8,64,128]{3,2,1,0:T(8,128)(2,1)} %get-tuple-element.53), channel_id=1, source_target_pairs={{0,48},{16,0},{32,16},{48,32},{1,49},{17,1},{33,17},{49,33},{2,50}... | collective-permute-start | bytes 1572872 | tf_op jit(solution)/shard_map/ppermute | solution.py:295
  43.8 1.0 collective-permute-start.3
  45.5 6.7 %shard_map.100.refs_5_ = bf16[8,8,72,128]{3,2,1,0:T(8,128)(2,1)} custom-call(s32[4]{0:T(128)} %pad_add_fusion.1.info, s32[8]{0:T(128)} %lengths.9, bf16[8,8,64,128]{3,2,1,0:T(8,128)(2,1)} %bitcast.7.refs_0_, bf16[8,512,1024]{2,1,0:T(8,128)(2,1)} %refs_1_.5, bf16[4,512,1024]{2,1,0:T(8,128)(2,1)} %collective-permute-done.1.refs_2_.refs_3_, ...), custom_call_target="tpu_custom_call" | custom-call | flops 1073741824 | bytes 2097152 | tf_op jit(solution)/shard_map/pallas_call | solution.py:147
  52.8 9.9 %shard_map.101 = (bf16[4,8,72,128]{3,2,1,0:T(8,128)(2,1)}, bf16[4,8,72,128]{3,2,1,0:T(8,128)(2,1)}) custom-call(s32[4]{0:T(128)} %pad_add_fusion.1.info, s32[8]{0:T(128)} %lengths.9, bf16[4,8,64,128]{3,2,1,0:T(8,128)(2,1)} %collective-permute-done.4.refs_0_, bf16[4,8,64,128]{3,2,1,0:T(8,128)(2,1)} %collective-permute-done.5.refs_1_, ...), custom_call_target="tpu_custom_call" | custom-call | flops 2147483648 | bytes 4194304 | tf_op jit(solution)/shard_map/pallas_call | solution.py:147
  62.7 1.7 %collective-permute-start.8 = (bf16[32,72,128]{2,1,0:T(8,128)(2,1)}, bf16[32,72,128]{2,1,0:T(8,128)(2,1)S(1)}, u32[]{:S(2)}, u32[]{:S(2)}) collective-permute-start(bf16[32,72,128]{2,1,0:T(8,128)(2,1)} %bitcast.46), channel_id=1, source_target_pairs={{0,6},{2,0},{4,2},{6,4},{1,7},{3,1},{5,3},{7,5},{8,14},{10,8},{12,... | collective-permute-start | bytes 1769480 | tf_op jit(solution)/shard_map/ppermute | solution.py:295
  64.3 3.4 %collective-permute-start.9 = (bf16[32,72,128]{2,1,0:T(8,128)(2,1)}, bf16[32,72,128]{2,1,0:T(8,128)(2,1)S(1)}, u32[]{:S(2)}, u32[]{:S(2)}) collective-permute-start(bf16[32,72,128]{2,1,0:T(8,128)(2,1)} %bitcast.45), channel_id=1, source_target_pairs={{0,48},{16,0},{32,16},{48,32},{1,49},{17,1},{33,17},{49,33},{2,50}... | collective-permute-start | bytes 1769480 | tf_op jit(solution)/shard_map/ppermute | solution.py:295
  67.7 9.9 %shard_map.102 = (bf16[4,8,72,128]{3,2,1,0:T(8,128)(2,1)}, bf16[4,8,72,128]{3,2,1,0:T(8,128)(2,1)}) custom-call(s32[4]{0:T(128)} %pad_add_fusion.1.info, s32[8]{0:T(128)} %lengths.9, bf16[4,8,64,128]{3,2,1,0:T(8,128)(2,1)} %copy-done.3, bf16[4,8,64,128]{3,2,1,0:T(8,128)(2,1)} %copy-done.4, bf16[8,512,1024]{2,1,0:T(8,128)(2,1)} %refs_1_.5, ...), custom_call_target="tpu_custom_call" | custom-call | flops 2147483648 | bytes 4194304 | tf_op jit(solution)/shard_map/pallas_call | solution.py:147
  77.9 9.9 %shard_map.103 = (bf16[4,8,72,128]{3,2,1,0:T(8,128)(2,1)}, bf16[4,8,72,128]{3,2,1,0:T(8,128)(2,1)}) custom-call(s32[4]{0:T(128)} %pad_add_fusion.1.info, s32[8]{0:T(128)} %lengths.9, bf16[8,8,64,128]{3,2,1,0:T(8,128)(2,1)} %collective-permute-done.3.refs_0_, bf16[8,512,1024]{2,1,0:T(8,128)(2,1)} %refs_1_.5, ...), custom_call_target="tpu_custom_call" | custom-call | flops 2147483648 | bytes 4194304 | tf_op jit(solution)/shard_map/pallas_call | solution.py:147
  87.8 1.1 collective-permute-start.12
  88.9 6.5 %shard_map.104 = bf16[8,8,72,128]{3,2,1,0:T(8,128)(2,1)} custom-call(s32[4]{0:T(128)} %pad_add_fusion.1.info, s32[8]{0:T(128)} %lengths.9, bf16[8,8,64,128]{3,2,1,0:T(8,128)(2,1)} %bitcast.7.refs_0_, bf16[8,512,1024]{2,1,0:T(8,128)(2,1)} %refs_1_.5, bf16[4,512,1024]{2,1,0:T(8,128)(2,1)} %collective-permute-done.1.refs_2_.refs_3_, ...), custom_call_target="tpu_custom_call", output_to_operand_aliasing={{}: (7, {})} | custom-call | flops 1073741824 | bytes 2097152 | tf_op jit(solution)/shard_map/pallas_call | solution.py:147
  95.4 7.1 %collective-permute-done.12.refs_4_ = bf16[32,72,128]{2,1,0:T(8,128)(2,1)} collective-permute-done((bf16[32,72,128]{2,1,0:T(8,128)(2,1)}, bf16[32,72,128]{2,1,0:T(8,128)(2,1)}, u32[]{:S(2)}, u32[]{:S(2)}) %collective-permute-start.12) | collective-permute-done | bytes 589856 | tf_op jit(solution)/shard_map/ppermute | solution.py:295
  102.5 4.1 %shard_map.105 = bf16[64,72,128]{2,1,0:T(8,128)(2,1)} custom-call(bf16[32,72,128]{2,1,0:T(8,128)(2,1)S(1)} %collective-permute-done.8.refs_0_, bf16[32,72,128]{2,1,0:T(8,128)(2,1)S(1)} %collective-permute-done.9.refs_1_, bf16[32,72,128]{2,1,0:T(8,128)(2,1)} %collective-permute-done.10.refs_2_, bf16[32,72,128]{2,1,0:T(8,128)(2,1)} %copy-done.2, ...), custom_call_target="tpu_custom_call" | custom-call | flops 4718592 | bytes 5898240 | tf_op jit(solution)/shard_map/pallas_call | solution.py:232
  106.6 10.5 %all-to-all-start.1 = ((bf16[64,72,128]{2,1,0:T(8,128)(2,1)}), bf16[64,72,128]{2,1,0:T(8,128)(2,1)S(1)}, u32[]{:S(2)}, u32[]{:S(2)}) async-start(bf16[64,72,128]{2,1,0:T(8,128)(2,1)} %shard_map.105), calls=%async_computation.1 | async-start | bytes 2359296 | tf_op jit(solution)/shard_map/all_to_all | solution.py:370
  117.1 1.9 %collective-permute-start.14 = (s32[4,8]{1,0:T(4,128)S(1)}, s32[4,8]{1,0:T(4,128)S(1)}, u32[]{:S(2)}, u32[]{:S(2)}) collective-permute-start(s32[4,8]{1,0:T(4,128)S(1)} %get-tuple-element.64), channel_id=1, source_target_pairs={{0,8},{8,0},{1,9},{9,1},{2,10},{10,2},{3,11},{11,3},{4,12},{12,4},... | collective-permute-start | bytes 392 | tf_op jit(solution)/shard_map/ppermute | solution.py:318
  121.0 1.1 copy.14.value_ref
  122.1 1.2 fusion.2
  123.6 10.4 %all-to-all-done.1.x_ref = bf16[64,72,128]{2,1,0:T(8,128)(2,1)S(1)} async-done(((bf16[64,72,128]{2,1,0:T(8,128)(2,1)}), bf16[64,72,128]{2,1,0:T(8,128)(2,1)S(1)}, u32[]{:S(2)}, u32[]{:S(2)}) %all-to-all-start.1) | async-done | bytes 1179680 | tf_op jit(solution)/shard_map/all_to_all | solution.py:370
  134.5 3.8 %collective-permute-start.15 = (bf16[4,4,8,128]{3,2,1,0:T(8,128)(2,1)S(1)}, bf16[4,4,8,128]{3,2,1,0:T(8,128)(2,1)S(1)}, u32[]{:S(2)}, u32[]{:S(2)}) collective-permute-start(bf16[4,4,8,128]{3,2,1,0:T(8,128)(2,1)S(1)} %get-tuple-element.56), channel_id=1, source_target_pairs={{0,8},{8,0},{1,9},{9,1},{2,10},{10,2},{3,11},{11,3},{4,12},{12,4},... | collective-permute-start | bytes 98312 | tf_op jit(solution)/shard_map/ppermute | solution.py:389
  (58 shorter events, 8.8 us)
Async XLA Ops:
  0.0 119.9 %copy-start = (bf16[1024,1024]{1,0:T(8,128)(2,1)S(1)}, bf16[1024,1024]{1,0:T(8,128)(2,1)}, u32[]{:S(2)}) copy-start(bf16[1024,1024]{1,0:T(8,128)(2,1)} %param.14) | copy-start | bytes 6291460
  0.9 4.9 %copy-start.8 = (pred[64]{0:T(512)(128)(4,1)S(1)}, pred[64]{0:T(512)(128)(4,1)}, u32[]{:S(2)}) copy-start(pred[64]{0:T(512)(128)(4,1)} %constant.62) | copy-start | bytes 196
  1.0 5.2 %copy-start.1 = (bf16[8,512,1024]{2,1,0:T(8,128)(2,1)S(1)}, bf16[8,512,1024]{2,1,0:T(8,128)(2,1)}, u32[]{:S(2)}) copy-start(bf16[8,512,1024]{2,1,0:T(8,128)(2,1)} %refs_3_.5) | copy-start | bytes 25165828
  1.0 4.9 %collective-permute-start = (bf16[4,4,8,128]{3,2,1,0:T(8,128)(2,1)S(1)}, bf16[4,4,8,128]{3,2,1,0:T(8,128)(2,1)S(1)}, u32[]{:S(2)}, u32[]{:S(2)}) collective-permute-start(bf16[4,4,8,128]{3,2,1,0:T(8,128)(2,1)S(1)} %get-tuple-element.29), channel_id=1, source_target_pairs={{0,8},{8,0},{1,9},{9,1},{2,10},{10,2},{3,11},{11,3},{4,12},{12,4},... | collective-permute-start | bytes 98312 | tf_op jit(solution)/shard_map/ppermute | solution.py:317
  5.7 30.5 %collective-permute-start.1 = (bf16[4,512,1024]{2,1,0:T(8,128)(2,1)S(1)}, bf16[4,512,1024]{2,1,0:T(8,128)(2,1)}, u32[]{:S(2)}, u32[]{:S(2)}) collective-permute-start(bf16[4,512,1024]{2,1,0:T(8,128)(2,1)S(1)} %constant_dynamic-slice_fusion.3), channel_id=1, source_target_pairs={{0,8},{8,0},{1,9},{9,1},{2,10},{10,2},{3,11},{11,3},{4,12},{12,4},... | collective-permute-start | bytes 12582920 | tf_op jit(solution)/shard_map/ppermute | solution.py:337
  6.7 29.6 %collective-permute-start.2 = (bf16[4,512,1024]{2,1,0:T(8,128)(2,1)S(1)}, bf16[4,512,1024]{2,1,0:T(8,128)(2,1)}, u32[]{:S(2)}, u32[]{:S(2)}) collective-permute-start(bf16[4,512,1024]{2,1,0:T(8,128)(2,1)S(1)} %constant_dynamic-slice_fusion.2), channel_id=1, source_target_pairs={{0,8},{8,0},{1,9},{9,1},{2,10},{10,2},{3,11},{11,3},{4,12},{12,4},... | collective-permute-start | bytes 12582920 | tf_op jit(solution)/shard_map/ppermute | solution.py:338
  38.5 13.7 %collective-permute-start.4 = (bf16[4,8,64,128]{3,2,1,0:T(8,128)(2,1)}, bf16[4,8,64,128]{3,2,1,0:T(8,128)(2,1)}, u32[]{:S(2)}, u32[]{:S(2)}) collective-permute-start(bf16[4,8,64,128]{3,2,1,0:T(8,128)(2,1)} %get-tuple-element.54), channel_id=1, source_target_pairs={{0,2},{2,4},{4,6},{6,0},{1,3},{3,5},{5,7},{7,1},{8,10},{10,12},{12... | collective-permute-start | bytes 1572872 | tf_op jit(solution)/shard_map/ppermute | solution.py:295
  39.1 13.1 %collective-permute-start.5 = (bf16[4,8,64,128]{3,2,1,0:T(8,128)(2,1)}, bf16[4,8,64,128]{3,2,1,0:T(8,128)(2,1)}, u32[]{:S(2)}, u32[]{:S(2)}) collective-permute-start(bf16[4,8,64,128]{3,2,1,0:T(8,128)(2,1)} %get-tuple-element.53), channel_id=1, source_target_pairs={{0,16},{16,32},{32,48},{48,0},{1,17},{17,33},{33,49},{49,1},{2,18}... | collective-permute-start | bytes 1572872 | tf_op jit(solution)/shard_map/ppermute | solution.py:295
  39.5 12.7 %collective-permute-start.6 = (bf16[4,8,64,128]{3,2,1,0:T(8,128)(2,1)}, bf16[4,8,64,128]{3,2,1,0:T(8,128)(2,1)S(1)}, u32[]{:S(2)}, u32[]{:S(2)}) collective-permute-start(bf16[4,8,64,128]{3,2,1,0:T(8,128)(2,1)} %get-tuple-element.54), channel_id=1, source_target_pairs={{0,6},{2,0},{4,2},{6,4},{1,7},{3,1},{5,3},{7,5},{8,14},{10,8},{12,... | collective-permute-start | bytes 1572872 | tf_op jit(solution)/shard_map/ppermute | solution.py:295
  41.6 11.2 %collective-permute-start.7 = (bf16[4,8,64,128]{3,2,1,0:T(8,128)(2,1)}, bf16[4,8,64,128]{3,2,1,0:T(8,128)(2,1)S(1)}, u32[]{:S(2)}, u32[]{:S(2)}) collective-permute-start(bf16[4,8,64,128]{3,2,1,0:T(8,128)(2,1)} %get-tuple-element.53), channel_id=1, source_target_pairs={{0,48},{16,0},{32,16},{48,32},{1,49},{17,1},{33,17},{49,33},{2,50}... | collective-permute-start | bytes 1572872 | tf_op jit(solution)/shard_map/ppermute | solution.py:295
  43.8 34.1 %collective-permute-start.3 = (bf16[8,8,64,128]{3,2,1,0:T(8,128)(2,1)}, bf16[8,8,64,128]{3,2,1,0:T(8,128)(2,1)}, u32[]{:S(2)}, u32[]{:S(2)}) collective-permute-start(bf16[8,8,64,128]{3,2,1,0:T(8,128)(2,1)} %bitcast.7.refs_0_), channel_id=1, source_target_pairs={{0,1},{64,65},{1,0},{65,64},{2,3},{66,67},{3,2},{67,66},{4,5},{68,... | collective-permute-start | bytes 3145736 | tf_op jit(solution)/shard_map/ppermute | solution.py:293
  52.2 10.5 %copy-start.3 = (bf16[4,8,64,128]{3,2,1,0:T(8,128)(2,1)}, bf16[4,8,64,128]{3,2,1,0:T(8,128)(2,1)S(1)}, u32[]{:S(2)}) copy-start(bf16[4,8,64,128]{3,2,1,0:T(8,128)(2,1)S(1)} %collective-permute-done.6.refs_0_) | copy-start | bytes 1572868
  52.8 9.9 %copy-start.4 = (bf16[4,8,64,128]{3,2,1,0:T(8,128)(2,1)}, bf16[4,8,64,128]{3,2,1,0:T(8,128)(2,1)S(1)}, u32[]{:S(2)}) copy-start(bf16[4,8,64,128]{3,2,1,0:T(8,128)(2,1)S(1)} %collective-permute-done.7.refs_1_) | copy-start | bytes 1572868
  62.7 15.2 %collective-permute-start.8 = (bf16[32,72,128]{2,1,0:T(8,128)(2,1)}, bf16[32,72,128]{2,1,0:T(8,128)(2,1)S(1)}, u32[]{:S(2)}, u32[]{:S(2)}) collective-permute-start(bf16[32,72,128]{2,1,0:T(8,128)(2,1)} %bitcast.46), channel_id=1, source_target_pairs={{0,6},{2,0},{4,2},{6,4},{1,7},{3,1},{5,3},{7,5},{8,14},{10,8},{12,... | collective-permute-start | bytes 1769480 | tf_op jit(solution)/shard_map/ppermute | solution.py:295
  64.3 13.6 %collective-permute-start.9 = (bf16[32,72,128]{2,1,0:T(8,128)(2,1)}, bf16[32,72,128]{2,1,0:T(8,128)(2,1)S(1)}, u32[]{:S(2)}, u32[]{:S(2)}) collective-permute-start(bf16[32,72,128]{2,1,0:T(8,128)(2,1)} %bitcast.45), channel_id=1, source_target_pairs={{0,48},{16,0},{32,16},{48,32},{1,49},{17,1},{33,17},{49,33},{2,50}... | collective-permute-start | bytes 1769480 | tf_op jit(solution)/shard_map/ppermute | solution.py:295
  77.6 17.7 %collective-permute-start.10 = (bf16[32,72,128]{2,1,0:T(8,128)(2,1)}, bf16[32,72,128]{2,1,0:T(8,128)(2,1)}, u32[]{:S(2)}, u32[]{:S(2)}) collective-permute-start(bf16[32,72,128]{2,1,0:T(8,128)(2,1)} %bitcast.44), channel_id=1, source_target_pairs={{0,2},{2,4},{4,6},{6,0},{1,3},{3,5},{5,7},{7,1},{8,10},{10,12},{12... | collective-permute-start | bytes 1769480 | tf_op jit(solution)/shard_map/ppermute | solution.py:295
  77.6 17.7 %collective-permute-start.11 = (bf16[32,72,128]{2,1,0:T(8,128)(2,1)}, bf16[32,72,128]{2,1,0:T(8,128)(2,1)S(1)}, u32[]{:S(2)}, u32[]{:S(2)}) collective-permute-start(bf16[32,72,128]{2,1,0:T(8,128)(2,1)} %bitcast.43), channel_id=1, source_target_pairs={{0,16},{16,32},{32,48},{48,0},{1,17},{17,33},{33,49},{49,1},{2,18}... | collective-permute-start | bytes 1769480 | tf_op jit(solution)/shard_map/ppermute | solution.py:295
  87.8 14.7 %collective-permute-start.12 = (bf16[32,72,128]{2,1,0:T(8,128)(2,1)}, bf16[32,72,128]{2,1,0:T(8,128)(2,1)}, u32[]{:S(2)}, u32[]{:S(2)}) collective-permute-start(bf16[32,72,128]{2,1,0:T(8,128)(2,1)} %bitcast.48), channel_id=1, source_target_pairs={{0,4},{2,6},{4,0},{6,2},{1,5},{3,7},{5,1},{7,3},{8,12},{10,14},{12... | collective-permute-start | bytes 1769480 | tf_op jit(solution)/shard_map/ppermute | solution.py:295
  88.9 13.6 %collective-permute-start.13 = (bf16[32,72,128]{2,1,0:T(8,128)(2,1)}, bf16[32,72,128]{2,1,0:T(8,128)(2,1)}, u32[]{:S(2)}, u32[]{:S(2)}) collective-permute-start(bf16[32,72,128]{2,1,0:T(8,128)(2,1)} %bitcast.47), channel_id=1, source_target_pairs={{0,1},{64,65},{1,0},{65,64},{2,3},{66,67},{3,2},{67,66},{4,5},{68,... | collective-permute-start | bytes 1769480 | tf_op jit(solution)/shard_map/ppermute | solution.py:293
  95.4 21.7 %copy-start.5 = (s32[8,8]{1,0:T(8,128)S(1)}, s32[8,8]{1,0:T(8,128)}, u32[]{:S(2)}) copy-start(s32[8,8]{1,0:T(8,128)} %param.16) | copy-start | bytes 772
  95.4 7.1 %copy-start.2 = (bf16[32,72,128]{2,1,0:T(8,128)(2,1)}, bf16[32,72,128]{2,1,0:T(8,128)(2,1)S(1)}, u32[]{:S(2)}) copy-start(bf16[32,72,128]{2,1,0:T(8,128)(2,1)S(1)} %collective-permute-done.11.refs_3_) | copy-start | bytes 1769476
  106.6 27.4 %all-to-all-start.1 = ((bf16[64,72,128]{2,1,0:T(8,128)(2,1)}), bf16[64,72,128]{2,1,0:T(8,128)(2,1)S(1)}, u32[]{:S(2)}, u32[]{:S(2)}) async-start(bf16[64,72,128]{2,1,0:T(8,128)(2,1)} %shard_map.105), calls=%async_computation.1 | async-start | bytes 2359296 | tf_op jit(solution)/shard_map/all_to_all | solution.py:370
  117.1 2.8 %collective-permute-start.14 = (s32[4,8]{1,0:T(4,128)S(1)}, s32[4,8]{1,0:T(4,128)S(1)}, u32[]{:S(2)}, u32[]{:S(2)}) collective-permute-start(s32[4,8]{1,0:T(4,128)S(1)} %get-tuple-element.64), channel_id=1, source_target_pairs={{0,8},{8,0},{1,9},{9,1},{2,10},{10,2},{3,11},{11,3},{4,12},{12,4},... | collective-permute-start | bytes 392 | tf_op jit(solution)/shard_map/ppermute | solution.py:318
  134.5 4.7 %collective-permute-start.15 = (bf16[4,4,8,128]{3,2,1,0:T(8,128)(2,1)S(1)}, bf16[4,4,8,128]{3,2,1,0:T(8,128)(2,1)S(1)}, u32[]{:S(2)}, u32[]{:S(2)}) collective-permute-start(bf16[4,4,8,128]{3,2,1,0:T(8,128)(2,1)S(1)} %get-tuple-element.56), channel_id=1, source_target_pairs={{0,8},{8,0},{1,9},{9,1},{2,10},{10,2},{3,11},{11,3},{4,12},{12,4},... | collective-permute-start | bytes 98312 | tf_op jit(solution)/shard_map/ppermute | solution.py:389
  (2 other events, 9.9 us)
